TPU v7x, 256 devices: a whole 4x4x8 slice. The times are simulated.
256 devices in a mesh: expert: 64 (over y, z, core), dp: 4 (over x).
Axes of the slice: x: 4, y: 4, z: 8, core: 2. Of those that a mesh axis runs over, the one named last changes fastest.
Arguments:
- tokens: bfloat16 [32768, 1440], P(('expert', 'dp')), may hold values from -6 to 6
- routes: int32 [32768, 4], P(('expert', 'dp')), may hold values from 0 to 63, as said below
- gate_fixed: int32 [32768, 4], P(('expert', 'dp')), may hold values from 4096 to 65535
- counts: int32 [256], P(('expert', 'dp')), may hold values from 32 to 128, as said below
- replica_plan: int32 [8], replicated, may hold values from 0 to 63, as said below
- weight_in: bfloat16 [64, 1440, 1440], P('expert', None, 'dp'), may hold values from -0.15625 to 0.15625
- weight_out: bfloat16 [64, 1440, 1440], P('expert', 'dp'), may hold values from -0.15625 to 0.15625
- cotangent: bfloat16 [32768, 1440], P(('expert', 'dp')), may hold values from -0.59765625 to 0.59765625
Outputs:
- layer_output: bfloat16 [32768, 1440], P(('expert', 'dp'))
- input_grads: bfloat16 [32768, 1440], P(('expert', 'dp'))
- weight_in_grad: bfloat16 [64, 1440, 1440], P('expert', None, 'dp')
- weight_out_grad: bfloat16 [64, 1440, 1440], P('expert', 'dp')
Inputs may be any that keep to these rules, and one draw needn't show every extreme that they name: `routes`: each row names 4 different experts. `replica_plan`: 8 different experts, among them 0, 31, 32 and 63, in any order. `counts`: some device has 128 live tokens in every draw.
All inputs are finite; a program needn't handle non-finite values.
Results may differ from a plain program's by a relative error of at most 0.0064.
Values may be sent and summed in bfloat16 or wider, within the bound.
No kernel may reach another device: no remote copies, remote signals or barrier semaphores. Data moves between devices by JAX's collectives and lax.ppermute only.
A program may use at most 128 MiB of HBM per device.

v0:
```python
import jax
import jax.numpy as jnp
from jax import lax
from jax.sharding import PartitionSpec as P


def shifted(value, axis, steps):
    count = lax.axis_size(axis)
    pairs = [(source, (source + steps) % count) for source in range(count)]
    return lax.ppermute(value, axis, pairs)


def activate(values):
    return values * jax.nn.sigmoid(1.702 * values)


def derivative(values):
    sigmoid_value = jax.nn.sigmoid(1.702 * values)
    return sigmoid_value + 1.702 * values * sigmoid_value * (1.0 - sigmoid_value)


def slot_tables(routes, live_count, frequent_indicator, experts, capacity, spare_slots):
    token_count, top_count = routes.shape
    slot_width = capacity + spare_slots
    active = (jnp.arange(token_count, dtype=jnp.int32) < live_count).astype(jnp.int32)
    flattened = routes.reshape(-1)
    active_flat = jnp.repeat(active, top_count, total_repeat_length=token_count * top_count)
    same_expert = (flattened[:, None] == jnp.arange(experts, dtype=jnp.int32)[None, :]).astype(
        jnp.int32
    )
    matches = same_expert * active_flat[:, None]
    before = jnp.cumsum(matches, axis=0) - matches
    position = jnp.sum(before * matches, axis=1)
    hot_route = jnp.sum(same_expert * frequent_indicator[None, :], axis=1)
    keep_route = (active_flat > 0) & (position < capacity + spare_slots * hot_route)
    target_block = jnp.where(position < capacity, flattened, (flattened + experts // 2) % experts)
    slot_index = jnp.where(keep_route, target_block * slot_width + position, experts * slot_width)
    source = jnp.full((experts * slot_width + 1,), -1, jnp.int32)
    source = source.at[slot_index].set(jnp.arange(token_count * top_count, dtype=jnp.int32))
    return (slot_index, source[: experts * slot_width])


def gather_back(returned, slot_index, features):
    flattened = returned.reshape(-1, features)
    padded = jnp.concatenate([flattened, jnp.zeros((1, features), flattened.dtype)], axis=0)
    return padded[slot_index].astype(jnp.float32)


def slot_products(stacked, own_weight, copy_weight, dims, capacity, amount):
    width = stacked.shape[2]
    own_part = stacked[:, :capacity].reshape(-1, width)
    copy_part = stacked[:, capacity:].reshape(-1, width)
    own_term = lax.dot_general(own_part, own_weight, dims, preferred_element_type=jnp.float32)
    copy_term = lax.dot_general(copy_part, copy_weight, dims, preferred_element_type=jnp.float32)
    return jnp.concatenate(
        [
            own_term.reshape(amount, capacity, -1),
            copy_term.reshape(amount, stacked.shape[1] - capacity, -1),
        ],
        axis=1,
    )


def on_device(tokens, routes, gate_fixed, counts, replica_plan, weight_in, weight_out, cotangent):
    token_count, features = tokens.shape
    top_count = routes.shape[1]
    groups = lax.axis_size("expert")
    experts = groups * weight_in.shape[0]
    capacity = 3 * token_count * top_count // (8 * experts)
    spare_slots = capacity // 2
    slot_width = capacity + spare_slots
    contract_first = (((0,), (0,)), ((), ()))
    contract_last = (((1,), (1,)), ((), ()))
    contract_plain = (((1,), (0,)), ((), ()))
    frequent_indicator = jnp.sum(
        (replica_plan[:, None] == jnp.arange(experts, dtype=jnp.int32)[None, :]).astype(jnp.int32),
        axis=0,
    )
    slot_index, source = slot_tables(
        routes, counts[0], frequent_indicator, experts, capacity, spare_slots
    )
    filled = (source >= 0)[:, None]
    route_ids = jnp.maximum(source, 0)
    token_ids = route_ids // top_count
    scales = gate_fixed.reshape(-1).astype(jnp.float32) / 65536.0
    sent_rows = jnp.where(filled, tokens[token_ids], jnp.zeros((), jnp.bfloat16)).reshape(
        experts, slot_width, features
    )
    grad_rows = jnp.where(
        filled, scales[route_ids][:, None] * cotangent[token_ids].astype(jnp.float32), 0.0
    )
    grad_rows = grad_rows.astype(jnp.bfloat16).reshape(experts, slot_width, features)
    slab_in, slab_out = shifted((weight_in, weight_out), "expert", groups // 2)
    w_first = weight_in[0]
    w_second = weight_out[0]
    copy_first = slab_in[0]
    copy_second = slab_out[0]
    inbound = lax.all_to_all(sent_rows, "expert", split_axis=0, concat_axis=0, tiled=True)
    all_in = lax.all_gather(inbound, "dp", axis=0, tiled=True)
    blocks = all_in.shape[0]
    own_rows = all_in[:, :capacity].reshape(-1, features)
    copy_rows = all_in[:, capacity:].reshape(-1, features)
    own_pre = jnp.dot(own_rows, w_first, preferred_element_type=jnp.float32)
    copy_pre = jnp.dot(copy_rows, copy_first, preferred_element_type=jnp.float32)
    own_act = activate(own_pre).astype(jnp.bfloat16)
    copy_act = activate(copy_pre).astype(jnp.bfloat16)
    hidden_share = own_act.shape[1]
    act_all = jnp.concatenate(
        [
            own_act.reshape(blocks, capacity, hidden_share),
            copy_act.reshape(blocks, spare_slots, hidden_share),
        ],
        axis=1,
    )
    outputs = lax.psum_scatter(
        slot_products(
            act_all, w_second, copy_second, contract_plain, capacity, groups * lax.axis_size("dp")
        ),
        "dp",
        scatter_dimension=0,
        tiled=True,
    ).astype(jnp.bfloat16)
    returned = lax.all_to_all(outputs, "expert", split_axis=0, concat_axis=0, tiled=True)
    inbound_grad = lax.all_to_all(grad_rows, "expert", split_axis=0, concat_axis=0, tiled=True)
    all_grad = lax.all_gather(inbound_grad, "dp", axis=0, tiled=True)
    own_grad = all_grad[:, :capacity].reshape(-1, features)
    copy_grad = all_grad[:, capacity:].reshape(-1, features)
    own_act_grad = lax.dot_general(
        own_grad, w_second, contract_last, preferred_element_type=jnp.float32
    )
    copy_act_grad = lax.dot_general(
        copy_grad, copy_second, contract_last, preferred_element_type=jnp.float32
    )
    own_pre_grad = (own_act_grad * derivative(own_pre)).astype(jnp.bfloat16)
    copy_pre_grad = (copy_act_grad * derivative(copy_pre)).astype(jnp.bfloat16)
    pre_all = jnp.concatenate(
        [
            own_pre_grad.reshape(blocks, capacity, hidden_share),
            copy_pre_grad.reshape(blocks, spare_slots, hidden_share),
        ],
        axis=1,
    )
    input_rows = lax.psum_scatter(
        slot_products(
            pre_all, w_first, copy_first, contract_last, capacity, groups * lax.axis_size("dp")
        ),
        "dp",
        scatter_dimension=0,
        tiled=True,
    ).astype(jnp.bfloat16)
    copy_term_second = lax.dot_general(
        copy_act, copy_grad, contract_first, preferred_element_type=jnp.float32
    )
    copy_term_first = lax.dot_general(
        copy_rows, copy_pre_grad, contract_first, preferred_element_type=jnp.float32
    )
    home_second, home_first = (
        shifted(copy_term_second.astype(jnp.bfloat16), "expert", groups // 2).astype(
            copy_term_second.dtype
        ),
        shifted(copy_term_first.astype(jnp.bfloat16), "expert", groups // 2).astype(
            copy_term_first.dtype
        ),
    )
    grad_second = (
        lax.dot_general(own_act, own_grad, contract_first, preferred_element_type=jnp.float32)
        + home_second
    )
    grad_first = (
        lax.dot_general(own_rows, own_pre_grad, contract_first, preferred_element_type=jnp.float32)
        + home_first
    )
    weight_out_grad = grad_second.astype(jnp.bfloat16)[None]
    weight_in_grad = grad_first.astype(jnp.bfloat16)[None]
    returned_grad = lax.all_to_all(input_rows, "expert", split_axis=0, concat_axis=0, tiled=True)
    picked = gather_back(returned, slot_index, features) * scales[:, None]
    layer_output = jnp.sum(picked.reshape(token_count, top_count, features), axis=1).astype(
        jnp.bfloat16
    )
    picked_grad = gather_back(returned_grad, slot_index, features)
    input_grads = jnp.sum(picked_grad.reshape(token_count, top_count, features), axis=1).astype(
        jnp.bfloat16
    )
    return (layer_output, input_grads, weight_in_grad, weight_out_grad)


def solution(mesh):
    return jax.shard_map(
        on_device,
        mesh=mesh,
        in_specs=(
            P(("expert", "dp"), None),
            P(("expert", "dp"), None),
            P(("expert", "dp"), None),
            P(("expert", "dp")),
            P(),
            P("expert", None, "dp"),
            P("expert", "dp", None),
            P(("expert", "dp"), None),
        ),
        out_specs=(
            P(("expert", "dp"), None),
            P(("expert", "dp"), None),
            P("expert", None, "dp"),
            P("expert", "dp", None),
        ),
        check_vma=False,
    )
```

profile of v0, /device:TPU:1, one launch (start us, length us, event | category | flops | bytes accessed | tf_op | source)
XLA Modules:
  0.0 530.6 jit_solution(11869775184831770626)
XLA Ops:
  7.9 0.8 add_add_fusion.1
  8.7 3.3 gather_fusion
  12.8 1.2 reduce-window.14
  14.4 2.4 scatter_custom_fusion
  17.3 1.9 gather_fusion.3
  19.6 1.3 gather_fusion.4
  20.8 0.5 reshape.323
  21.3 0.4 select_convert_fusion
  21.8 36.2 %all_to_all.20 = bf16[64,4,1440]{2,1,0:T(4,128)(2,1)} all-to-all(bf16[64,4,1440]{2,1,0:T(4,128)(2,1)S(1)} %select_convert_fusion), channel_id=1, replica_groups=mesh['expert'=64,'dp'=4] {'expert'}, dimensions={0} | all-to-all | bytes 1474560 | tf_op jit(solution)/shard_map/all_to_all | solution.py:124
  58.2 1.3 gather_fusion.1
  59.7 0.4 broadcast_select_fusion
  60.1 29.1 %all_to_all.21 = bf16[64,4,1440]{2,1,0:T(4,128)(2,1)} all-to-all(bf16[64,4,1440]{2,1,0:T(4,128)(2,1)S(1)} %broadcast_select_fusion), channel_id=1, replica_groups=mesh['expert'=64,'dp'=4] {'expert'}, dimensions={0} | all-to-all | bytes 1474560 | tf_op jit(solution)/shard_map/all_to_all | solution.py:98
  89.2 2.9 collective-permute-start
  92.3 0.6 dynamic-slice.6
  93.5 3.5 all-gather.5.cloned.1.call-done
  97.1 3.6 slice.60
  100.7 3.3 copy.76
  104.0 37.2 %all-gather.3.cloned.1.call-done = bf16[256,4,1440]{2,1,0:T(4,128)(2,1)} async-done(((bf16[64,4,1440]{2,1,0:T(4,128)(2,1)}), bf16[256,4,1440]{2,1,0:T(4,128)(2,1)}) %all-gather.3.cloned.1.call-update) | async-done | bytes 2949136 | tf_op jit(solution)/shard_map/all_gather | solution.py:99
  141.2 4.9 slice.58
  146.1 4.6 copy.75
  150.7 4.1 reshape.318
  154.8 5.4 %reshape.314 = bf16[768,1440]{1,0:T(8,128)(2,1)S(1)} reshape(bf16[256,3,1440]{2,1,0:T(4,128)(2,1)} %bitcast.86) | data formatting | bytes 4423680 | tf_op jit(solution)/shard_map/reshape | solution.py:101
  160.2 3.3 multiply_convert_fusion
  163.6 2.6 fusion
  166.2 0.3 copy.67
  166.5 0.5 copy-done.9
  167.0 0.3 copy.59
  167.3 0.3 dot_general.41
  167.7 0.3 dot_general.46
  168.0 0.4 copy-done.1
  168.4 1.8 fusion.11
  170.3 2.7 fusion.6
  172.9 1.7 fusion.1
  174.7 1.8 convolution_bitcast_fusion
  176.5 2.9 pad_maximum_fusion.1
  179.4 7.9 %copy.70 = f32[256,4,1440]{2,1,0:T(4,128)} copy(f32[256,4,1440]{0,2,1:T(8,128)} %pad_maximum_fusion.1) | data formatting | bytes 11796480 | tf_op jit(solution)/shard_map/concatenate | solution.py:55
  187.3 2.6 fusion.4
  189.9 1.9 convolution_bitcast_fusion.1
  191.8 2.9 pad_maximum_fusion
  194.7 7.8 %copy.63 = f32[256,4,1440]{2,1,0:T(4,128)} copy(f32[256,4,1440]{0,2,1:T(8,128)} %pad_maximum_fusion) | data formatting | bytes 11796480 | tf_op jit(solution)/shard_map/concatenate | solution.py:55
  202.5 215.7 %all-reduce.6 = (bf16[256,4,1440]{2,1,0:T(4,128)(2,1)}, bf16[256,4,1440]{2,1,0:T(4,128)(2,1)}) all-reduce(f32[256,4,1440]{2,1,0:T(4,128)} %copy.63, f32[256,4,1440]{2,1,0:T(4,128)} %copy.70), channel_id=2, replica_groups=mesh['expert'=64,'dp'=4] {'dp'}, use_global_device_ids=true, to_apply=%region_6.7.clone | all-reduce | flops 2949120 | bytes 17694720
  418.2 2.3 dynamic-slice_convert_fusion.1
  420.4 12.4 %all-to-all-start.1 = ((bf16[64,4,1440]{2,1,0:T(4,128)(2,1)}), bf16[64,4,1440]{2,1,0:T(4,128)(2,1)S(1)}, u32[]{:S(2)}, u32[]{:S(2)}) async-start(bf16[64,4,1440]{2,1,0:T(4,128)(2,1)} %dynamic-slice_convert_fusion.1), calls=%async_computation.1 | async-start | bytes 1572864 | tf_op jit(solution)/shard_map/all_to_all | solution.py:123
  432.8 1.5 convolution_convert_fusion.1
  434.3 3.0 collective-permute-start.3
  437.3 2.3 dynamic-slice_convert_fusion
  439.6 16.1 %all-to-all-done.1 = bf16[64,4,1440]{2,1,0:T(4,128)(2,1)S(1)} async-done(((bf16[64,4,1440]{2,1,0:T(4,128)(2,1)}), bf16[64,4,1440]{2,1,0:T(4,128)(2,1)S(1)}, u32[]{:S(2)}, u32[]{:S(2)}) %all-to-all-start.1) | async-done | bytes 737312 | tf_op jit(solution)/shard_map/all_to_all | solution.py:123
  455.8 6.2 %all-to-all-start.3 = ((bf16[64,4,1440]{2,1,0:T(4,128)(2,1)}), bf16[64,4,1440]{2,1,0:T(4,128)(2,1)S(1)}, u32[]{:S(2)}, u32[]{:S(2)}) async-start(bf16[64,4,1440]{2,1,0:T(4,128)(2,1)} %dynamic-slice_convert_fusion), calls=%async_computation.3 | async-start | bytes 1572864 | tf_op jit(solution)/shard_map/all_to_all | solution.py:175
  462.0 0.6 convolution_convert_fusion
  462.6 3.1 collective-permute-start.2
  465.7 4.0 collective-permute-done.3
  469.7 4.0 fusion.3
  473.7 27.4 %collective-permute-done.2 = bf16[1440,360]{1,0:T(8,128)(2,1)S(1)} collective-permute-done((bf16[1440,360]{1,0:T(8,128)(2,1)S(1)}, bf16[1440,360]{1,0:T(8,128)(2,1)S(1)}, u32[]{:S(2)}, u32[]{:S(2)}) %collective-permute-start.2) | collective-permute-done | bytes 1036832 | tf_op jit(solution)/shard_map/ppermute | solution.py:10
  501.1 2.4 fusion.2
  503.5 0.4 reshape.317
  504.0 0.4 reshape.321
  504.4 3.2 gather_fusion.5
  507.6 2.9 gather.36
  510.5 2.2 reduce_sum.55
  512.7 0.9 copy.72
  513.6 3.0 gather_fusion.2
  516.6 2.9 reshape.322
  519.5 3.1 multiply_reduce_fusion
  522.6 0.9 copy.71
  (79 shorter events, 2.7 us)
Async XLA Ops:
  7.2 4.9 copy-start.15
  7.2 5.0 copy-start.16
  7.2 5.5 %copy-start.18 = (s32[8]{0:T(128)S(1)}, s32[8]{0:T(128)}, u32[]{:S(2)}) copy-start(s32[8]{0:T(128)} %param.14) | copy-start | bytes 100
  7.2 89.9 %all-gather.5.cloned.1.call-start = ((), (), s32[]{:S(2)}) async-start(), calls=%async_computation.5 | async-start | bytes 3932160 | tf_op jit(solution)/shard_map/all_gather | solution.py:125
  8.7 8.2 %copy-start.17 = (s32[128,4]{0,1:T(4,128)S(1)}, s32[128,4]{0,1:T(4,128)}, u32[]{:S(2)}) copy-start(s32[128,4]{0,1:T(4,128)} %param.12) | copy-start | bytes 6148
  12.1 7.3 %copy-start.13 = (bf16[128,1440]{0,1:T(8,128)(2,1)S(1)}, bf16[128,1440]{0,1:T(8,128)(2,1)}, u32[]{:S(2)}) copy-start(bf16[128,1440]{0,1:T(8,128)(2,1)} %param.17) | copy-start | bytes 1105924
  17.1 2.2 copy-start.8
  21.8 36.3 %copy-start.14 = (bf16[128,1440]{0,1:T(8,128)(2,1)S(1)}, bf16[128,1440]{0,1:T(8,128)(2,1)}, u32[]{:S(2)}) copy-start(bf16[128,1440]{0,1:T(8,128)(2,1)} %param.10) | copy-start | bytes 1105924
  58.0 83.2 %all-gather.3.cloned.1.call-start = ((), (), s32[]{:S(2)}) async-start(), calls=%async_computation.4 | async-start | bytes 3932160 | tf_op jit(solution)/shard_map/all_gather | solution.py:99
  60.1 32.2 %copy-start.19 = (u32[256]{0:T(256)S(1)}, u32[256]{0:T(256)}, u32[]{:S(2)}) copy-start(u32[256]{0:T(256)} %constant.170) | copy-start | bytes 3076
  89.2 78.8 %collective-permute-start = (bf16[1,1440,360]{2,1,0:T(8,128)(2,1)}, bf16[1,1440,360]{2,1,0:T(8,128)(2,1)}, u32[]{:S(2)}, u32[]{:S(2)}) collective-permute-start(bf16[1,1440,360]{2,1,0:T(8,128)(2,1)} %param.15), channel_id=1, source_target_pairs={{0,128},{4,132},{8,136},{12,140},{16,144},{20,148},{24,152},{28,15... | collective-permute-start | bytes 3110408 | tf_op jit(solution)/shard_map/ppermute | solution.py:10
  92.1 80.8 %collective-permute-start.1 = (bf16[1,360,1440]{2,1,0:T(8,128)(2,1)}, bf16[1,360,1440]{2,1,0:T(8,128)(2,1)}, u32[]{:S(2)}, u32[]{:S(2)}) collective-permute-start(bf16[1,360,1440]{2,1,0:T(8,128)(2,1)} %param.16), channel_id=1, source_target_pairs={{0,128},{4,132},{8,136},{12,140},{16,144},{20,148},{24,152},{28,15... | collective-permute-start | bytes 3110408 | tf_op jit(solution)/shard_map/ppermute | solution.py:10
  141.2 9.5 %copy-start = (bf16[256,4,1440]{2,1,0:T(4,128)(2,1)S(1)}, bf16[256,4,1440]{2,1,0:T(4,128)(2,1)}, u32[]{:S(2)}) copy-start(bf16[256,4,1440]{2,1,0:T(4,128)(2,1)} %all-gather.5.cloned.1.call-done) | copy-start | bytes 8847364
  160.2 3.3 copy-start.2
  160.2 3.4 copy-start.4
  163.5 3.0 copy-start.11
  166.2 0.8 copy-start.9
  167.3 1.1 copy-start.1
  170.2 2.7 copy-start.5
  174.6 4.8 copy-start.6
  420.4 35.3 %all-to-all-start.1 = ((bf16[64,4,1440]{2,1,0:T(4,128)(2,1)}), bf16[64,4,1440]{2,1,0:T(4,128)(2,1)S(1)}, u32[]{:S(2)}, u32[]{:S(2)}) async-start(bf16[64,4,1440]{2,1,0:T(4,128)(2,1)} %dynamic-slice_convert_fusion.1), calls=%async_computation.1 | async-start | bytes 1572864 | tf_op jit(solution)/shard_map/all_to_all | solution.py:123
  434.3 35.4 %collective-permute-start.3 = (bf16[360,1440]{1,0:T(8,128)(2,1)}, bf16[360,1440]{1,0:T(8,128)(2,1)}, u32[]{:S(2)}, u32[]{:S(2)}) collective-permute-start(bf16[360,1440]{1,0:T(8,128)(2,1)} %convolution_convert_fusion.1), channel_id=1, source_target_pairs={{0,128},{4,132},{8,136},{12,140},{16,144},{20,148},{24,152},{28,15... | collective-permute-start | bytes 3110408 | tf_op jit(solution)/shard_map/ppermute | solution.py:10
  437.3 24.7 %copy-start.7 = (bf16[256,360]{0,1:T(8,128)(2,1)S(1)}, bf16[256,360]{0,1:T(8,128)(2,1)}, u32[]{:S(2)}) copy-start(bf16[256,360]{0,1:T(8,128)(2,1)} %copy-done.6) | copy-start | bytes 552964
  439.6 30.0 %copy-start.12 = (bf16[768,360]{0,1:T(8,128)(2,1)S(1)}, bf16[768,360]{0,1:T(8,128)(2,1)}, u32[]{:S(2)}) copy-start(bf16[768,360]{0,1:T(8,128)(2,1)} %copy-done.11) | copy-start | bytes 1658884
  455.8 48.2 %all-to-all-start.3 = ((bf16[64,4,1440]{2,1,0:T(4,128)(2,1)}), bf16[64,4,1440]{2,1,0:T(4,128)(2,1)S(1)}, u32[]{:S(2)}, u32[]{:S(2)}) async-start(bf16[64,4,1440]{2,1,0:T(4,128)(2,1)} %dynamic-slice_convert_fusion), calls=%async_computation.3 | async-start | bytes 1572864 | tf_op jit(solution)/shard_map/all_to_all | solution.py:175
  462.6 38.5 %collective-permute-start.2 = (bf16[1440,360]{1,0:T(8,128)(2,1)S(1)}, bf16[1440,360]{1,0:T(8,128)(2,1)S(1)}, u32[]{:S(2)}, u32[]{:S(2)}) collective-permute-start(bf16[1440,360]{1,0:T(8,128)(2,1)S(1)} %convolution_convert_fusion), channel_id=1, source_target_pairs={{0,128},{4,132},{8,136},{12,140},{16,144},{20,148},{24,152},{28,15... | collective-permute-start | bytes 3110408 | tf_op jit(solution)/shard_map/ppermute | solution.py:10
  465.7 35.4 %copy-start.3 = (bf16[768,1440]{1,0:T(8,128)(2,1)S(1)}, bf16[768,1440]{1,0:T(8,128)(2,1)}, u32[]{:S(2)}) copy-start(bf16[768,1440]{1,0:T(8,128)(2,1)} %copy-done.2) | copy-start | bytes 6635524
  465.7 35.4 %copy-start.10 = (bf16[768,360]{0,1:T(8,128)(2,1)S(1)}, bf16[768,360]{0,1:T(8,128)(2,1)}, u32[]{:S(2)}) copy-start(bf16[768,360]{0,1:T(8,128)(2,1)} %copy-done.9) | copy-start | bytes 1658884
Sparse Core Ops, SparseCore 0:
  58.1 38.9 all-gather.4
  98.9 42.2 all-gather.2
where the time goes:
time: 540 us; the launch traced here: 531 us
  blocking collectives  281 us (52%)
  waiting for transfers between devices  88.3 us (16%)
  local copies, waits for them, and re-layouts  76.1 us (14%)
  starting transfers between devices  27.8 us (5%)
  matrix products  27 us (5%)
  between operations  16.2 us (3%)
  other arithmetic  14.4 us (3%)
    unnamed x1, blocking collectives  216 us
    all_gather x1, waiting for transfers between devices, on_device(): all_in = lax.all_gather(inbound, 'dp', axis=0, tiled=True)  37.2 us
    all_to_all x1, blocking collectives, on_device(): lax.all_to_all(grad_rows, 'expert', split_axis=0, concat_axis=0, tiled=True)  36.2 us
    ppermute x4, waiting for transfers between devices, shifted(): return lax.ppermute(value, axis, pairs)  31.4 us
    all_to_all x1, blocking collectives, on_device(): lax.all_to_all(sent_rows, 'expert', split_axis=0, concat_axis=0, tiled=True)  29.1 us
    all_to_all x1, waiting for transfers between devices, on_device(): lax.all_to_all(outputs, 'expert', split_axis=0, concat_axis=0, tiled=True)  16.1 us
    concatenate x2, local copies, waits for them, and re-layouts, slot_products(): jnp.concatenate([own_term.reshape(amount, capacity, -1), copy_term.reshap...  15.7 us
    all_to_all x1, starting transfers between devices, on_device(): lax.all_to_all(outputs, 'expert', split_axis=0, concat_axis=0, tiled=True)  12.4 us
  transfers between devices with their start and end apart: 8, of which 5 were waited for; matrix products, arithmetic and copies ran while one was open for 10% of the time, Pallas kernels for 0%

commit v1 on v0

--- a/solution.py
+++ b/solution.py
@@ -2,6 +2,11 @@
 import jax.numpy as jnp
 from jax import lax
 from jax.sharding import PartitionSpec as P
+
+
+def gather_over(shard, axis, along):
+    sent = jnp.stack([shard] * lax.axis_size(axis))
+    return jnp.concatenate(lax.all_to_all(sent, axis, 0, 0), axis=along)
 
 
 def shifted(value, axis, steps):
@@ -96,7 +101,7 @@
     copy_first = slab_in[0]
     copy_second = slab_out[0]
     inbound = lax.all_to_all(sent_rows, "expert", split_axis=0, concat_axis=0, tiled=True)
-    all_in = lax.all_gather(inbound, "dp", axis=0, tiled=True)
+    all_in = gather_over(inbound, "dp", 0)
     blocks = all_in.shape[0]
     own_rows = all_in[:, :capacity].reshape(-1, features)
     copy_rows = all_in[:, capacity:].reshape(-1, features)

time: 540 us -> 567 us (1.050)
  blocking collectives: 281 us -> 216 us
  waiting for transfers between devices: 88.3 us -> 135 us
  starting transfers between devices: 27.8 us -> 52.2 us
  local copies, waits for them, and re-layouts: 76.1 us -> 90.3 us
    all_to_all x0 -> x3, waiting for transfers between devices: none -> 87.1 us  [the longest x1 44.8 us: gather_over(): return jnp.concatenate(lax.all_to_all(sent, axis, 0, 0), axis=along)]
    all_to_all x2 -> x0, blocking collectives: 65.3 us -> none  [the longest x1 36.2 us: on_device(): lax.all_to_all(grad_rows, 'expert', split_axis=0, concat_axis=0, tiled=True)]
    all_gather x1 -> x0, waiting for transfers between devices: 37.2 us -> none  [on_device(): all_in = lax.all_gather(inbound, 'dp', axis=0, tiled=True)]
    all_to_all x0 -> x3, starting transfers between devices: none -> 24.1 us  [the longest x1 13.2 us: on_device(): lax.all_to_all(grad_rows, 'expert', split_axis=0, concat_axis=0, tiled=True)]
    unnamed x48 -> x39, local copies, waits for them, and re-layouts: 11.8 us -> 8.22 us
  transfers between devices with their start and end apart: 8 -> 10, of which waited for: 5 -> 6; matrix products, arithmetic and copies ran while one was open for 10% -> 10% of each run, Pallas kernels for 0% -> 0%
where the time goes in v1:
time: 567 us; the launch traced here: 558 us
  blocking collectives  216 us (38%)
  waiting for transfers between devices  135 us (24%)
  local copies, waits for them, and re-layouts  90.3 us (16%)
  starting transfers between devices  52.2 us (9%)
  matrix products  31 us (5%)
  other arithmetic  16.1 us (3%)
  between operations  16.1 us (3%)
    unnamed x1, blocking collectives  216 us
    all_to_all x1, waiting for transfers between devices, gather_over(): return jnp.concatenate(lax.all_to_all(sent, axis, 0, 0), axis=along)  44.8 us
    ppermute x4, waiting for transfers between devices, shifted(): return lax.ppermute(value, axis, pairs)  32.8 us
    all_to_all x1, waiting for transfers between devices, on_device(): lax.all_to_all(sent_rows, 'expert', split_axis=0, concat_axis=0, tiled=True)  22.2 us
    all_to_all x1, waiting for transfers between devices, on_device(): lax.all_to_all(grad_rows, 'expert', split_axis=0, concat_axis=0, tiled=True)  20 us
    concatenate x2, local copies, waits for them, and re-layouts, slot_products(): jnp.concatenate([own_term.reshape(amount, capacity, -1), copy_term.reshap...  15.7 us
    all_to_all x1, waiting for transfers between devices, on_device(): lax.all_to_all(outputs, 'expert', split_axis=0, concat_axis=0, tiled=True)  15 us
    all_to_all x1, starting transfers between devices, on_device(): lax.all_to_all(grad_rows, 'expert', split_axis=0, concat_axis=0, tiled=True)  13.2 us
  transfers between devices with their start and end apart: 10, of which 6 were waited for; matrix products, arithmetic and copies ran while one was open for 10% of the time, Pallas kernels for 0%

profile of v1, /device:TPU:1, one launch (start us, length us, event | category | flops | bytes accessed | tf_op | source)
XLA Modules:
  0.0 557.6 jit_solution(2185654271285743948)
XLA Ops:
  7.9 0.8 add_add_fusion.1
  8.7 3.3 gather_fusion
  12.7 1.2 reduce-window.14
  14.4 2.4 scatter_custom_fusion
  17.3 1.9 gather_fusion.3
  19.5 1.3 gather_fusion.4
  21.3 1.3 select_convert_fusion
  22.6 13.2 %all-to-all-start.3 = ((bf16[64,4,1440]{2,1,0:T(4,128)(2,1)}), bf16[64,4,1440]{2,1,0:T(4,128)(2,1)S(1)}, u32[]{:S(2)}, u32[]{:S(2)}) async-start(bf16[64,4,1440]{2,1,0:T(4,128)(2,1)} %select_convert_fusion), calls=%async_computation.3 | async-start | bytes 1572864 | tf_op jit(solution)/shard_map/all_to_all | solution.py:129
  36.0 1.3 gather_fusion.1
  37.4 1.3 broadcast_select_fusion
  38.8 20.0 %all-to-all-done.3 = bf16[64,4,1440]{2,1,0:T(4,128)(2,1)S(1)} async-done(((bf16[64,4,1440]{2,1,0:T(4,128)(2,1)}), bf16[64,4,1440]{2,1,0:T(4,128)(2,1)S(1)}, u32[]{:S(2)}, u32[]{:S(2)}) %all-to-all-start.3) | async-done | bytes 737312 | tf_op jit(solution)/shard_map/all_to_all | solution.py:129
  58.8 6.2 %all-to-all-start = ((bf16[64,4,1440]{2,1,0:T(4,128)(2,1)}), bf16[64,4,1440]{2,1,0:T(4,128)(2,1)S(1)}, u32[]{:S(2)}, u32[]{:S(2)}) async-start(bf16[64,4,1440]{2,1,0:T(4,128)(2,1)} %broadcast_select_fusion), calls=%async_computation | async-start | bytes 1572864 | tf_op jit(solution)/shard_map/all_to_all | solution.py:103
  65.0 0.7 all-gather.2.cloned.1.call-update
  65.7 22.2 %all-to-all-done = bf16[64,4,1440]{2,1,0:T(4,128)(2,1)S(1)} async-done(((bf16[64,4,1440]{2,1,0:T(4,128)(2,1)}), bf16[64,4,1440]{2,1,0:T(4,128)(2,1)S(1)}, u32[]{:S(2)}, u32[]{:S(2)}) %all-to-all-start) | async-done | bytes 737312 | tf_op jit(solution)/shard_map/all_to_all | solution.py:103
  88.1 2.0 stack.2
  90.1 4.8 all-to-all-start.1
  94.9 2.9 collective-permute-start
  99.6 44.8 %all-to-all-done.1 = bf16[4,64,4,1440]{3,1,2,0:T(8,128)(2,1)} async-done(((bf16[4,64,4,1440]{3,1,2,0:T(8,128)(2,1)}), bf16[4,64,4,1440]{3,1,2,0:T(8,128)(2,1)}, u32[]{:S(2)}, u32[]{:S(2)}) %all-to-all-start.1) | async-done | bytes 2949152 | tf_op jit(solution)/shard_map/all_to_all | solution.py:9
  144.4 2.2 copy.83
  146.8 3.7 copy.84
  150.4 6.7 %reshape.320 = bf16[768,1440]{1,0:T(8,128)(2,1)} reshape(bf16[256,3,1440]{2,1,0:T(4,128)(2,1)} %copy.84) | data formatting | bytes 4423680 | tf_op jit(solution)/shard_map/reshape | solution.py:106
  157.1 4.3 multiply_convert_fusion
  161.5 2.1 copy.85
  163.6 2.0 dot_general.41
  165.6 1.8 fusion.11
  167.5 2.0 convolution_bitcast_fusion.1
  169.5 2.6 fusion.4
  172.1 2.9 pad_maximum_fusion
  175.0 7.9 %copy.89 = f32[256,4,1440]{2,1,0:T(4,128)} copy(f32[256,4,1440]{0,2,1:T(8,128)} %pad_maximum_fusion) | data formatting | bytes 11796480 | tf_op jit(solution)/shard_map/concatenate | solution.py:60
  182.9 4.7 slice.60
  187.6 4.6 copy.101
  192.1 6.7 %reshape.324 = bf16[768,1440]{1,0:T(8,128)(2,1)} reshape(bf16[256,3,1440]{2,1,0:T(4,128)(2,1)} %bitcast.89) | data formatting | bytes 4423680 | tf_op jit(solution)/shard_map/reshape | solution.py:131
  198.9 4.3 fusion
  203.2 2.1 copy.93
  205.3 2.0 dot_general.46
  207.3 2.9 fusion.6
  210.2 1.7 fusion.1
  211.9 0.7 copy-done.4
  212.6 1.8 convolution_bitcast_fusion
  214.4 2.9 pad_maximum_fusion.1
  217.2 7.9 %copy.96 = f32[256,4,1440]{2,1,0:T(4,128)} copy(f32[256,4,1440]{0,2,1:T(8,128)} %pad_maximum_fusion.1) | data formatting | bytes 11796480 | tf_op jit(solution)/shard_map/concatenate | solution.py:60
  225.1 216.5 %all-reduce.6 = (bf16[256,4,1440]{2,1,0:T(4,128)(2,1)}, bf16[256,4,1440]{2,1,0:T(4,128)(2,1)}) all-reduce(f32[256,4,1440]{2,1,0:T(4,128)} %copy.89, f32[256,4,1440]{2,1,0:T(4,128)} %copy.96), channel_id=2, replica_groups=mesh['expert'=64,'dp'=4] {'dp'}, use_global_device_ids=true, to_apply=%region_6.7.clone | all-reduce | flops 2949120 | bytes 17694720
  441.6 2.3 dynamic-slice_convert_fusion.1
  443.8 12.1 %all-to-all-start.2 = ((bf16[64,4,1440]{2,1,0:T(4,128)(2,1)}), bf16[64,4,1440]{2,1,0:T(4,128)(2,1)}, u32[]{:S(2)}, u32[]{:S(2)}) async-start(bf16[64,4,1440]{2,1,0:T(4,128)(2,1)} %dynamic-slice_convert_fusion.1), calls=%async_computation.2 | async-start | bytes 1572864 | tf_op jit(solution)/shard_map/all_to_all | solution.py:128
  455.9 2.6 convolution_convert_fusion.1
  458.5 3.0 collective-permute-start.3
  461.5 2.4 dynamic-slice_convert_fusion
  463.9 15.0 %all-to-all-done.2 = bf16[64,4,1440]{2,1,0:T(4,128)(2,1)} async-done(((bf16[64,4,1440]{2,1,0:T(4,128)(2,1)}), bf16[64,4,1440]{2,1,0:T(4,128)(2,1)}, u32[]{:S(2)}, u32[]{:S(2)}) %all-to-all-start.2) | async-done | bytes 737312 | tf_op jit(solution)/shard_map/all_to_all | solution.py:128
  478.8 6.4 %all-to-all-start.4 = ((bf16[64,4,1440]{2,1,0:T(4,128)(2,1)}), bf16[64,4,1440]{2,1,0:T(4,128)(2,1)}, u32[]{:S(2)}, u32[]{:S(2)}) async-start(bf16[64,4,1440]{2,1,0:T(4,128)(2,1)} %dynamic-slice_convert_fusion), calls=%async_computation.4 | async-start | bytes 1572864 | tf_op jit(solution)/shard_map/all_to_all | solution.py:180
  485.8 3.1 collective-permute-start.2
  488.9 5.9 %collective-permute-done.3 = bf16[360,1440]{1,0:T(8,128)(2,1)} collective-permute-done((bf16[360,1440]{1,0:T(8,128)(2,1)}, bf16[360,1440]{1,0:T(8,128)(2,1)}, u32[]{:S(2)}, u32[]{:S(2)}) %collective-permute-start.3) | collective-permute-done | bytes 1036832 | tf_op jit(solution)/shard_map/ppermute | solution.py:15
  494.8 4.0 fusion.3
  498.8 26.9 %collective-permute-done.2 = bf16[1440,360]{1,0:T(8,128)(2,1)S(1)} collective-permute-done((bf16[1440,360]{1,0:T(8,128)(2,1)S(1)}, bf16[1440,360]{1,0:T(8,128)(2,1)S(1)}, u32[]{:S(2)}, u32[]{:S(2)}) %collective-permute-start.2) | collective-permute-done | bytes 1036832 | tf_op jit(solution)/shard_map/ppermute | solution.py:15
  525.6 2.5 fusion.2
  528.1 1.8 reshape.323
  530.0 1.6 reshape.327
  531.6 3.0 gather_fusion.5
  534.6 2.9 gather.36
  537.5 2.2 reduce_sum.55
  539.7 0.9 copy.98
  540.6 3.0 gather_fusion.2
  543.5 2.9 reshape.328
  546.5 3.1 multiply_reduce_fusion
  549.6 0.9 copy.97
  (75 shorter events, 5.0 us)
Async XLA Ops:
  7.2 4.9 copy-start.11
  7.2 5.0 copy-start.12
  7.2 5.4 copy-start.14
  7.2 9.7 %copy-start.13 = (s32[128,4]{0,1:T(4,128)S(1)}, s32[128,4]{0,1:T(4,128)}, u32[]{:S(2)}) copy-start(s32[128,4]{0,1:T(4,128)} %param.12) | copy-start | bytes 6148
  12.0 7.3 %copy-start.9 = (bf16[128,1440]{0,1:T(8,128)(2,1)S(1)}, bf16[128,1440]{0,1:T(8,128)(2,1)}, u32[]{:S(2)}) copy-start(bf16[128,1440]{0,1:T(8,128)(2,1)} %param.17) | copy-start | bytes 1105924
  17.0 2.2 copy-start.6
  21.3 14.5 %copy-start.10 = (bf16[128,1440]{0,1:T(8,128)(2,1)S(1)}, bf16[128,1440]{0,1:T(8,128)(2,1)}, u32[]{:S(2)}) copy-start(bf16[128,1440]{0,1:T(8,128)(2,1)} %param.10) | copy-start | bytes 1105924
  22.6 36.1 %all-to-all-start.3 = ((bf16[64,4,1440]{2,1,0:T(4,128)(2,1)}), bf16[64,4,1440]{2,1,0:T(4,128)(2,1)S(1)}, u32[]{:S(2)}, u32[]{:S(2)}) async-start(bf16[64,4,1440]{2,1,0:T(4,128)(2,1)} %select_convert_fusion), calls=%async_computation.3 | async-start | bytes 1572864 | tf_op jit(solution)/shard_map/all_to_all | solution.py:129
  58.8 6.3 %copy-start = (bf16[64,4,1440]{2,1,0:T(4,128)(2,1)}, bf16[64,4,1440]{2,1,0:T(4,128)(2,1)S(1)}, u32[]{:S(2)}) copy-start(bf16[64,4,1440]{2,1,0:T(4,128)(2,1)S(1)} %all-to-all-done.3) | copy-start | bytes 2211844
  58.8 29.2 %all-to-all-start = ((bf16[64,4,1440]{2,1,0:T(4,128)(2,1)}), bf16[64,4,1440]{2,1,0:T(4,128)(2,1)S(1)}, u32[]{:S(2)}, u32[]{:S(2)}) async-start(bf16[64,4,1440]{2,1,0:T(4,128)(2,1)} %broadcast_select_fusion), calls=%async_computation | async-start | bytes 1572864 | tf_op jit(solution)/shard_map/all_to_all | solution.py:103
  65.0 117.9 %all-gather.2.cloned.1.call-start = ((), (), s32[]{:S(2)}) async-start(), calls=%async_computation.5 | async-start | bytes 3932160 | tf_op jit(solution)/shard_map/all_gather | solution.py:130
  90.1 8.3 %copy-start.15 = (u32[256]{0:T(256)S(1)}, u32[256]{0:T(256)}, u32[]{:S(2)}) copy-start(u32[256]{0:T(256)} %constant.170) | copy-start | bytes 3076
  90.1 54.3 %all-to-all-start.1 = ((bf16[4,64,4,1440]{3,1,2,0:T(8,128)(2,1)}), bf16[4,64,4,1440]{3,1,2,0:T(8,128)(2,1)}, u32[]{:S(2)}, u32[]{:S(2)}) async-start(bf16[4,64,4,1440]{3,1,2,0:T(8,128)(2,1)} %stack.2), calls=%async_computation.1 | async-start | bytes 6291456 | tf_op jit(solution)/shard_map/all_to_all | solution.py:9
  94.9 70.7 %collective-permute-start = (bf16[1,1440,360]{2,1,0:T(8,128)(2,1)}, bf16[1,1440,360]{2,1,0:T(8,128)(2,1)}, u32[]{:S(2)}, u32[]{:S(2)}) collective-permute-start(bf16[1,1440,360]{2,1,0:T(8,128)(2,1)} %param.15), channel_id=1, source_target_pairs={{0,128},{4,132},{8,136},{12,140},{16,144},{20,148},{24,152},{28,15... | collective-permute-start | bytes 3110408 | tf_op jit(solution)/shard_map/ppermute | solution.py:15
  97.8 69.7 %collective-permute-start.1 = (bf16[1,360,1440]{2,1,0:T(8,128)(2,1)}, bf16[1,360,1440]{2,1,0:T(8,128)(2,1)}, u32[]{:S(2)}, u32[]{:S(2)}) collective-permute-start(bf16[1,360,1440]{2,1,0:T(8,128)(2,1)} %param.16), channel_id=1, source_target_pairs={{0,128},{4,132},{8,136},{12,140},{16,144},{20,148},{24,152},{28,15... | collective-permute-start | bytes 3110408 | tf_op jit(solution)/shard_map/ppermute | solution.py:15
  167.5 2.0 copy-start.1
  207.3 2.9 copy-start.3
  211.9 0.7 copy-start.4
  443.8 35.0 %all-to-all-start.2 = ((bf16[64,4,1440]{2,1,0:T(4,128)(2,1)}), bf16[64,4,1440]{2,1,0:T(4,128)(2,1)}, u32[]{:S(2)}, u32[]{:S(2)}) async-start(bf16[64,4,1440]{2,1,0:T(4,128)(2,1)} %dynamic-slice_convert_fusion.1), calls=%async_computation.2 | async-start | bytes 1572864 | tf_op jit(solution)/shard_map/all_to_all | solution.py:128
  458.5 36.3 %collective-permute-start.3 = (bf16[360,1440]{1,0:T(8,128)(2,1)}, bf16[360,1440]{1,0:T(8,128)(2,1)}, u32[]{:S(2)}, u32[]{:S(2)}) collective-permute-start(bf16[360,1440]{1,0:T(8,128)(2,1)} %convolution_convert_fusion.1), channel_id=1, source_target_pairs={{0,128},{4,132},{8,136},{12,140},{16,144},{20,148},{24,152},{28,15... | collective-permute-start | bytes 3110408 | tf_op jit(solution)/shard_map/ppermute | solution.py:15
  461.5 23.7 %copy-start.5 = (bf16[256,360]{0,1:T(8,128)(2,1)S(1)}, bf16[256,360]{0,1:T(8,128)(2,1)}, u32[]{:S(2)}) copy-start(bf16[256,360]{0,1:T(8,128)(2,1)} %copy-done.4) | copy-start | bytes 552964
  478.8 51.1 %all-to-all-start.4 = ((bf16[64,4,1440]{2,1,0:T(4,128)(2,1)}), bf16[64,4,1440]{2,1,0:T(4,128)(2,1)}, u32[]{:S(2)}, u32[]{:S(2)}) async-start(bf16[64,4,1440]{2,1,0:T(4,128)(2,1)} %dynamic-slice_convert_fusion), calls=%async_computation.4 | async-start | bytes 1572864 | tf_op jit(solution)/shard_map/all_to_all | solution.py:180
  485.2 9.6 %copy-start.7 = (bf16[768,360]{0,1:T(8,128)(2,1)S(1)}, bf16[768,360]{0,1:T(8,128)(2,1)}, u32[]{:S(2)}) copy-start(bf16[768,360]{0,1:T(8,128)(2,1)} %get-tuple-element.32) | copy-start | bytes 1658884
  485.8 39.8 %collective-permute-start.2 = (bf16[1440,360]{1,0:T(8,128)(2,1)S(1)}, bf16[1440,360]{1,0:T(8,128)(2,1)S(1)}, u32[]{:S(2)}, u32[]{:S(2)}) collective-permute-start(bf16[1440,360]{1,0:T(8,128)(2,1)S(1)} %convolution_convert_fusion), channel_id=1, source_target_pairs={{0,128},{4,132},{8,136},{12,140},{16,144},{20,148},{24,152},{28,15... | collective-permute-start | bytes 3110408 | tf_op jit(solution)/shard_map/ppermute | solution.py:15
  488.9 36.7 %copy-start.2 = (bf16[768,1440]{1,0:T(8,128)(2,1)S(1)}, bf16[768,1440]{1,0:T(8,128)(2,1)}, u32[]{:S(2)}) copy-start(bf16[768,1440]{1,0:T(8,128)(2,1)} %reshape.320) | copy-start | bytes 6635524
  488.9 36.7 %copy-start.8 = (bf16[768,360]{0,1:T(8,128)(2,1)S(1)}, bf16[768,360]{0,1:T(8,128)(2,1)}, u32[]{:S(2)}) copy-start(bf16[768,360]{0,1:T(8,128)(2,1)} %fusion) | copy-start | bytes 1658884
Sparse Core Ops, SparseCore 0:
  67.6 54.1 all-gather.1
